TPU v7x, 512 devices: a whole 4x4x16 slice. The times are simulated.
512 devices in a mesh: gx: 64 (over z_lo, x, core), yz: 8 (over y, z_hi).
Axes of the slice: x: 4, y: 4, z: 16 (z_hi: 2, z_lo: 8; z = z_hi * 8 + z_lo), core: 2. Of those that a mesh axis runs over, the one named last changes fastest.
Arguments:
- solution: float32 [4, 512, 64, 3, 128], P(None, 'gx', 'yz'), may hold values from -6 to 6
- residual: float32 [4, 512, 64, 3, 128], P(None, 'gx', 'yz'), may hold values from -6 to 6
- direction: float32 [4, 512, 64, 3, 128], P(None, 'gx', 'yz'), may hold values from -6 to 6
- stiffness: float32 [512, 64, 128], P('gx', 'yz'), may hold values from 0.5 to 13.52
- coupling: float32 [512, 64, 128], P('gx', 'yz'), may hold values from 0.5 to 2
- lower_factor: float32 [64, 8, 384, 384], P('gx', 'yz'), may hold values from -0.122474487 to 1
- upper_factor: float32 [64, 8, 384, 384], P('gx', 'yz'), may hold values from -0.122474487 to 2, as said below
- pivot_order: int32 [64, 8, 384], P('gx', 'yz'), may hold values from 0 to 383, each once within a row
- coarse_basis: float32 [4, 512, 64, 128], P(None, 'gx', 'yz'), may hold values from 0.2 to 1
- coarse_inverse: float32 [64, 8, 12, 6144], P('gx', 'yz'), may hold values from -0.00024917498 to 0.009765625
- inner_prior: float32 [4], replicated, may hold values from 6291456 to 25165824
Outputs:
- solution_next: float32 [4, 512, 64, 3, 128], P(None, 'gx', 'yz')
- residual_next: float32 [4, 512, 64, 3, 128], P(None, 'gx', 'yz')
- direction_next: float32 [4, 512, 64, 3, 128], P(None, 'gx', 'yz')
- inner_next: float32 [4], replicated
Inputs may be any that keep to these rules, and one draw needn't show every extreme that they name: `upper_factor`: upper triangular with positive diagonal.
All inputs are finite; a program needn't handle non-finite values.
Results may differ from a plain program's by a relative error of at most 0.000067.
Values sent between devices are 32-bit elements; how exact they have to be, the bound alone decides.
No kernel may reach another device: no remote copies, remote signals or barrier semaphores. Data moves between devices by JAX's collectives and lax.ppermute only.
A program may use at most 64 MiB of HBM per device.

v0:
```python
import jax
import jax.numpy as jnp
from jax import lax
from jax.sharding import PartitionSpec as P

precise = lax.Precision.HIGHEST


def with_halo(cells, sides, width):
    for axis, dim in sides:
        count = lax.axis_size(axis)
        ends = count - 1
        head = lax.slice_in_dim(cells, 0, width, axis=dim)
        tail = lax.slice_in_dim(cells, cells.shape[dim] - width, cells.shape[dim], axis=dim)
        cells = jnp.concatenate(
            [
                lax.ppermute(tail, axis, [(i, (i + 1) % count) for i in range(ends)]),
                cells,
                lax.ppermute(head, axis, [((i + 1) % count, i) for i in range(ends)]),
            ],
            axis=dim,
        )
    return cells


def stencil(padded, scaled):
    zero_plane = jnp.zeros_like(scaled[..., :1])
    upward = jnp.concatenate([scaled[..., 1:], zero_plane], axis=4)
    downward = jnp.concatenate([zero_plane, scaled[..., :-1]], axis=4)
    beside = padded[:, 2:, 1:-1] + padded[:, :-2, 1:-1] + padded[:, 1:-1, 2:] + padded[:, 1:-1, :-2]
    return 6.0 * scaled - beside - upward - downward


def operate(direction, stiffness, coupling):
    scaled = stiffness[None, :, :, None, :] * direction
    padded = with_halo(scaled, (("gx", 1), ("yz", 2)), 1)
    return stiffness[None, :, :, None, :] * stencil(padded, scaled) + coupling[
        None, :, :, None, :
    ] * jnp.sum(direction, axis=3, keepdims=True)


def local_solve(field, lower_factor, upper_factor, pivot_order):
    line_width = lower_factor.shape[-1]
    line_rows = field.reshape(-1, line_width)
    pivots = pivot_order.reshape(line_width)
    inverse_order = jnp.argsort(pivots)
    permuted = jnp.take(line_rows, pivots, axis=1)
    middle = jnp.dot(
        permuted, lower_factor[0, 0].T, precision=precise, preferred_element_type=jnp.float32
    )
    solved = jnp.dot(
        middle, upper_factor[0, 0].T, precision=precise, preferred_element_type=jnp.float32
    )
    return jnp.take(solved, inverse_order, axis=1).reshape(field.shape)


def across(padded, field):
    field_shape = field.shape
    blank_rows = jnp.zeros(field_shape[:1] + (field_shape[1] - 2,) + field_shape[2:], field.dtype)
    across_first = jnp.concatenate([padded[:, :1, 1:-1], blank_rows, padded[:, -1:, 1:-1]], axis=1)
    blank_cols = jnp.zeros(field_shape[:2] + (field_shape[2] - 2,) + field_shape[3:], field.dtype)
    across_second = jnp.concatenate([padded[:, 1:-1, :1], blank_cols, padded[:, 1:-1, -1:]], axis=2)
    return field + 0.5 * (across_first + across_second)


def restrict(coarse_basis, field):
    weighted = jnp.einsum("pxyz,cxykz->ckp", coarse_basis, field, precision=precise)
    return weighted.reshape(field.shape[0], -1)


def prolong(coarse_basis, coarse_values, field_shape):
    shaped = coarse_values.reshape(field_shape[0], field_shape[3], coarse_basis.shape[0])
    return jnp.einsum("pxyz,ckp->cxykz", coarse_basis, shaped, precision=precise)


def per_device(
    solution,
    residual,
    direction,
    stiffness,
    coupling,
    lower_factor,
    upper_factor,
    pivot_order,
    coarse_basis,
    coarse_inverse,
    inner_prior,
):
    case_count = residual.shape[0]
    applied = operate(direction, stiffness, coupling)
    curve_part = jnp.sum(direction * applied, axis=(1, 2, 3, 4))
    curvature = lax.psum(curve_part, ("gx", "yz"))
    step_size = inner_prior / curvature
    step_field = step_size[:, None, None, None, None]
    residual_next = residual - step_field * applied
    primal = restrict(coarse_basis, residual_next)
    primal_all = lax.all_gather(primal[:, None, :], ("gx", "yz"), axis=1, tiled=True).reshape(
        case_count, -1
    )
    coarse_values = jnp.dot(
        primal_all, coarse_inverse[0, 0].T, precision=precise, preferred_element_type=jnp.float32
    )
    correction = prolong(coarse_basis, coarse_values, residual.shape)
    local_part = local_solve(residual_next, lower_factor, upper_factor, pivot_order)
    padded = with_halo(local_part, (("gx", 1), ("yz", 2)), 1)
    smoothed = across(padded, local_part)
    preconditioned = smoothed + correction
    inner_part = jnp.sum(residual_next * preconditioned, axis=(1, 2, 3, 4))
    inner_next = lax.psum(inner_part, ("gx", "yz"))
    growth = (inner_next / inner_prior)[:, None, None, None, None]
    direction_next = preconditioned + growth * direction
    solution_next = solution + step_field * direction
    return (solution_next, residual_next, direction_next, inner_next)


def solution(mesh):
    in_specs = (
        P(None, "gx", "yz", None, None),
        P(None, "gx", "yz", None, None),
        P(None, "gx", "yz", None, None),
        P("gx", "yz", None),
        P("gx", "yz", None),
        P("gx", "yz", None, None),
        P("gx", "yz", None, None),
        P("gx", "yz", None),
        P(None, "gx", "yz", None),
        P("gx", "yz", None, None),
        P(),
    )
    out_specs = (
        P(None, "gx", "yz", None, None),
        P(None, "gx", "yz", None, None),
        P(None, "gx", "yz", None, None),
        P(),
    )
    return jax.shard_map(
        per_device, mesh=mesh, in_specs=in_specs, out_specs=out_specs, check_vma=False
    )
```

profile of v0, /device:TPU:1, one launch (start us, length us, event | category | flops | bytes accessed | tf_op | source)
XLA Modules:
  0.0 2391.1 jit_solution(16158936149588700655)
XLA Ops:
  0.6 1.3 copy_multiply_fusion
  2.0 8.7 collective-permute-start
  10.8 2.1 collective-permute-start.1
  13.2 3.8 sort.17
  17.2 0.7 reduce.1
  18.1 11.2 collective-permute-start.3
  29.3 1.3 collective-permute-start.2
  30.6 3.7 collective-permute-done.3
  34.3 10.0 collective-permute-done.2
  44.3 0.7 multiply_reduce_fusion.1
  45.0 103.4 %psum.14 = f32[4]{0:T(128)S(1)} all-reduce(f32[4]{0:T(128)S(1)} %get-tuple-element.19), channel_id=1, replica_groups=mesh['gx'=64,'yz'=8] {'gx','yz'}, use_global_device_ids=true, to_apply=%region_2.0 | all-reduce | flops 4 | bytes 32 | tf_op jit(solution)/shard_map/psum | solution.py:92
  148.5 0.3 copy_subtract_fusion
  148.9 0.8 copy-done.8
  149.7 1.6 convolution_bitcast_fusion.1
  151.6 1.7 gather_fusion
  153.3 1.5 fusion.2
  154.8 0.8 fusion
  155.6 1.7 gather_fusion.1
  157.6 2.6 collective-permute-start.4
  160.2 2047.1 %all_gather.3 = f32[4,512,12]{2,0,1:T(4,128)S(1)} all-gather(f32[4,1,12]{2,0,1:T(4,128)S(1)} %broadcast_in_dim_reshape.3), channel_id=1, replica_groups=mesh['gx'=64,'yz'=8] {'gx','yz'}, dimensions={1}, use_global_device_ids=true | all-gather | bytes 98496 | tf_op jit(solution)/shard_map/all_gather | solution.py:97
  2207.4 0.7 reshape.66
  2208.1 1.9 collective-permute-start.5
  2210.4 15.4 collective-permute-done.5
  2225.8 1.3 collective-permute-start.7
  2227.1 12.9 collective-permute-start.6
  2240.0 3.3 convolution_bitcast_fusion.2
  2243.3 1.0 multiply_reduce_fusion
  2244.3 144.2 %psum.15 = f32[4]{0:T(128)S(1)} all-reduce(f32[4]{0:T(128)S(1)} %get-tuple-element.33), channel_id=1, replica_groups=mesh['gx'=64,'yz'=8] {'gx','yz'}, use_global_device_ids=true, to_apply=%region_5.7 | all-reduce | flops 4 | bytes 32 | tf_op jit(solution)/shard_map/psum | solution.py:109
  2388.5 0.5 copy-done.12
  2389.0 0.6 multiply_add_fusion
  2389.6 0.8 copy.69
  2390.4 0.8 copy.71
  (63 shorter events, 1.8 us)
Async XLA Ops:
  0.6 152.6 %copy-start = (f32[1,1,384,384]{3,2,1,0:T(8,128)S(1)}, f32[1,1,384,384]{3,2,1,0:T(8,128)}, u32[]{:S(2)}) copy-start(f32[1,1,384,384]{3,2,1,0:T(8,128)} %param.18) | copy-start | bytes 1769476
  2.0 16.1 collective-permute-start
  10.8 2.4 copy-start.10
  10.8 2.4 copy-start.1
  10.8 7.3 collective-permute-start.1
  13.2 3.8 copy-start.9
  13.2 3.9 copy-start.6
  18.1 26.2 %copy-start.7 = (f32[8,8,128]{2,1,0:T(8,128)S(1)}, f32[8,8,128]{2,1,0:T(8,128)}, u32[]{:S(2)}) copy-start(f32[8,8,128]{2,1,0:T(8,128)} %param.16) | copy-start | bytes 98308
  18.1 16.2 collective-permute-start.3
  29.3 15.0 collective-permute-start.2
  44.3 104.2 %copy-start.5 = (f32[4,8,8,3,128]{4,2,3,1,0:T(8,128)S(1)}, f32[4,8,8,3,128]{4,2,3,1,0:T(8,128)}, u32[]{:S(2)}) copy-start(f32[4,8,8,3,128]{4,2,3,1,0:T(8,128)} %param.14) | copy-start | bytes 1179652
  45.0 103.5 %copy-start.11 = (f32[4]{0:T(128)S(1)}, f32[4]{0:T(128)}, u32[]{:S(2)}) copy-start(f32[4]{0:T(128)} %param.23) | copy-start | bytes 52
  148.8 0.9 copy-start.8
  148.9 2.7 copy-start.2
  153.3 1.5 copy-start.3
  157.6 2052.4 %collective-permute-start.4 = (f32[4,1,8,3,128]{4,0,2,1,3:T(4,128)S(1)}, f32[4,1,8,3,128]{4,0,2,1,3:T(4,128)S(1)}, u32[]{:S(2)}, u32[]{:S(2)}) collective-permute-start(f32[4,1,8,3,128]{4,0,2,1,3:T(4,128)S(1)} %copy.96), channel_id=1, source_target_pairs={{0,8},{8,16},{16,24},{24,32},{32,40},{40,48},{48,56},{56,64},{64,7... | collective-permute-start | bytes 147464 | tf_op jit(solution)/shard_map/ppermute | solution.py:17
  2208.1 17.6 collective-permute-start.5
  2225.8 17.5 collective-permute-start.7
  2227.1 16.2 collective-permute-start.6
  2243.3 145.7 %copy-start.4 = (f32[4,8,8,3,128]{4,2,3,1,0:T(8,128)S(1)}, f32[4,8,8,3,128]{4,2,3,1,0:T(8,128)}, u32[]{:S(2)}) copy-start(f32[4,8,8,3,128]{4,2,3,1,0:T(8,128)} %param.13) | copy-start | bytes 1179652
  2388.5 0.5 copy-start.12
where the time goes:
time: 2390 us
  blocking collectives  2290 us (96%)
  starting transfers between devices  42 us (2%)
  waiting for transfers between devices  29.1 us (1%)
    all_gather x1, blocking collectives, per_device(): lax.all_gather(primal[:, None, :], ('gx', 'yz'), axis=1, tiled=True)  2050 us
    psum x1, blocking collectives, per_device(): inner_next = lax.psum(inner_part, ('gx', 'yz'))  144 us
    psum x1, blocking collectives, per_device(): curvature = lax.psum(curve_part, ('gx', 'yz'))  103 us
  transfers between devices with their start and end apart: 8, of which 3 were waited for; matrix products, arithmetic and copies ran while one was open for 0% of the time, Pallas kernels for 0%

commit v1 on v0

--- a/solution.py
+++ b/solution.py
@@ -106,7 +106,7 @@
     smoothed = across(padded, local_part)
     preconditioned = smoothed + correction
     inner_part = jnp.sum(residual_next * preconditioned, axis=(1, 2, 3, 4))
-    inner_next = lax.psum(inner_part, ("gx", "yz"))
+    inner_next = jnp.sum(lax.all_gather(inner_part, ("gx", "yz")), axis=0)
     growth = (inner_next / inner_prior)[:, None, None, None, None]
     direction_next = preconditioned + growth * direction
     solution_next = solution + step_field * direction

time: 2390 us -> 2390 us (level)
    psum x1 -> x0, blocking collectives: 144 us -> none  [per_device(): inner_next = lax.psum(inner_part, ('gx', 'yz'))]
    unnamed x0 -> x1, blocking collectives: none -> 144 us
where the time goes in v1:
time: 2390 us
  blocking collectives  2290 us (96%)
  starting transfers between devices  42 us (2%)
  waiting for transfers between devices  29.1 us (1%)
    all_gather x1, blocking collectives, per_device(): lax.all_gather(primal[:, None, :], ('gx', 'yz'), axis=1, tiled=True)  2050 us
    unnamed x1, blocking collectives  144 us
    psum x1, blocking collectives, per_device(): curvature = lax.psum(curve_part, ('gx', 'yz'))  103 us
  transfers between devices with their start and end apart: 8, of which 3 were waited for; matrix products, arithmetic and copies ran while one was open for 0% of the time, Pallas kernels for 0%

profile of v1, /device:TPU:1, one launch (start us, length us, event | category | flops | bytes accessed | tf_op | source)
XLA Modules:
  0.0 2391.8 jit_solution(15710393862742560780)
XLA Ops:
  0.6 1.3 copy_multiply_fusion
  2.0 8.7 collective-permute-start
  10.8 2.1 collective-permute-start.1
  13.2 3.8 sort.17
  17.2 0.7 reduce.1
  18.1 11.2 collective-permute-start.3
  29.3 1.3 collective-permute-start.2
  30.6 3.7 collective-permute-done.3
  34.3 10.0 collective-permute-done.2
  44.3 0.7 multiply_reduce_fusion.1
  45.0 103.4 %psum.7 = f32[4]{0:T(128)S(1)} all-reduce(f32[4]{0:T(128)S(1)} %get-tuple-element.19), channel_id=1, replica_groups=mesh['gx'=64,'yz'=8] {'gx','yz'}, use_global_device_ids=true, to_apply=%region_2.0 | all-reduce | flops 4 | bytes 32 | tf_op jit(solution)/shard_map/psum | solution.py:92
  148.5 0.3 copy_subtract_fusion
  148.9 0.8 copy-done.8
  149.7 1.6 convolution_bitcast_fusion.1
  151.6 1.7 gather_fusion
  153.3 1.5 fusion.2
  154.8 0.8 fusion
  155.6 1.7 gather_fusion.1
  157.6 2.6 collective-permute-start.4
  160.3 2047.0 %all_gather.9 = f32[4,512,12]{2,0,1:T(4,128)S(1)} all-gather(f32[4,1,12]{2,0,1:T(4,128)S(1)} %broadcast_in_dim_reshape.3), channel_id=1, replica_groups=mesh['gx'=64,'yz'=8] {'gx','yz'}, dimensions={1}, use_global_device_ids=true | all-gather | bytes 98496 | tf_op jit(solution)/shard_map/all_gather | solution.py:97
  2207.3 0.7 reshape.69
  2208.1 1.9 collective-permute-start.5
  2210.3 15.4 collective-permute-done.5
  2225.8 1.3 collective-permute-start.7
  2227.1 12.9 collective-permute-start.6
  2240.0 3.3 convolution_bitcast_fusion.2
  2243.3 1.0 multiply_reduce_fusion
  2244.6 144.2 %all-reduce.2 = f32[2048]{0:T(1024)S(1)} all-reduce(f32[2048]{0:T(1024)S(1)} %dynamic-update-slice), channel_id=2, replica_groups=mesh['gx'=64,'yz'=8] {'gx','yz'}, use_global_device_ids=true, to_apply=%add.2 | all-reduce | flops 2048 | bytes 16384
  2389.2 0.5 copy-done.11
  2389.6 0.6 multiply_add_fusion
  2390.2 0.8 copy.69
  2391.0 0.8 copy.71
  (67 shorter events, 2.4 us)
Async XLA Ops:
  0.6 152.7 %copy-start = (f32[1,1,384,384]{3,2,1,0:T(8,128)S(1)}, f32[1,1,384,384]{3,2,1,0:T(8,128)}, u32[]{:S(2)}) copy-start(f32[1,1,384,384]{3,2,1,0:T(8,128)} %param.18) | copy-start | bytes 1769476
  2.0 16.1 collective-permute-start
  10.8 2.4 copy-start.10
  10.8 2.4 copy-start.1
  10.8 7.3 collective-permute-start.1
  13.2 3.8 copy-start.9
  13.2 3.9 copy-start.6
  18.1 26.2 %copy-start.7 = (f32[8,8,128]{2,1,0:T(8,128)S(1)}, f32[8,8,128]{2,1,0:T(8,128)}, u32[]{:S(2)}) copy-start(f32[8,8,128]{2,1,0:T(8,128)} %param.16) | copy-start | bytes 98308
  18.1 16.2 collective-permute-start.3
  29.3 15.0 collective-permute-start.2
  44.3 104.2 %copy-start.5 = (f32[4,8,8,3,128]{4,2,3,1,0:T(8,128)S(1)}, f32[4,8,8,3,128]{4,2,3,1,0:T(8,128)}, u32[]{:S(2)}) copy-start(f32[4,8,8,3,128]{4,2,3,1,0:T(8,128)} %param.14) | copy-start | bytes 1179652
  45.0 103.5 %copy-start.12 = (f32[4]{0:T(128)S(1)}, f32[4]{0:T(128)}, u32[]{:S(2)}) copy-start(f32[4]{0:T(128)} %param.23) | copy-start | bytes 52
  148.8 0.9 copy-start.8
  148.9 2.7 copy-start.2
  153.3 1.5 copy-start.3
  157.6 2052.4 %collective-permute-start.4 = (f32[4,1,8,3,128]{4,0,2,1,3:T(4,128)S(1)}, f32[4,1,8,3,128]{4,0,2,1,3:T(4,128)S(1)}, u32[]{:S(2)}, u32[]{:S(2)}) collective-permute-start(f32[4,1,8,3,128]{4,0,2,1,3:T(4,128)S(1)} %copy.96), channel_id=1, source_target_pairs={{0,8},{8,16},{16,24},{24,32},{32,40},{40,48},{48,56},{56,64},{64,7... | collective-permute-start | bytes 147464 | tf_op jit(solution)/shard_map/ppermute | solution.py:17
  2208.1 17.7 collective-permute-start.5
  2225.8 17.5 collective-permute-start.7
  2227.1 16.2 collective-permute-start.6
  2244.3 145.3 %copy-start.4 = (f32[4,8,8,3,128]{4,2,3,1,0:T(8,128)S(1)}, f32[4,8,8,3,128]{4,2,3,1,0:T(8,128)}, u32[]{:S(2)}) copy-start(f32[4,8,8,3,128]{4,2,3,1,0:T(8,128)} %param.13) | copy-start | bytes 1179652
  2389.1 0.5 copy-start.11
